TPU v7x, 128 devices: a whole 4x4x4 slice. The times are simulated.
128 devices in a mesh: span: 8 (over z, core), xs: 16 (over y, x).
Axes of the slice: x: 4, y: 4, z: 4, core: 2. Of those that a mesh axis runs over, the one named last changes fastest.
Arguments:
- source: float32 [64, 64, 4096], P(None, 'span', 'xs'), may hold values from -0.75 to 0.75
- coefficient: float32 [64, 64, 4096], P(None, 'span', 'xs'), may hold values from 2.5 to 5
- volume_matrix: float32 [64, 64], replicated, may hold values from -0.75 to 0.75
- span_lower: float32 [64, 64], replicated, may hold values from -0.375 to 0.375
- span_upper: float32 [64, 64], replicated, may hold values from -0.375 to 0.375
- cross_lower: float32 [64, 64], replicated, may hold values from -0.375 to 0.375
- cross_upper: float32 [64, 64], replicated, may hold values from -0.375 to 0.375
- interface: int32 [8, 16, 128], P('span', 'xs'), may hold values from 0 to 131071
- compliance: float32 [8, 2048, 2048], P('span', 'xs'), may hold values from -0.5 to 0.5
- start_displacement: float32 [8, 16, 128], P('span', 'xs'), may hold values from -8 to 8
Outputs:
- fluid_state: float32 [64, 64, 4096], P(None, 'span', 'xs')
- shell_displacement: float32 [8, 16, 128], P('span', 'xs')
All inputs are finite; a program needn't handle non-finite values.
Results may differ from a plain program's by a relative error of at most 0.0001.
Values sent between devices are 32-bit elements; how exact they have to be, the bound alone decides.
No kernel may reach another device: no remote copies, remote signals or barrier semaphores. Data moves between devices by JAX's collectives and lax.ppermute only.
A program may use at most 64 MiB of HBM per device.

v0:
```python
import jax
import jax.numpy as jnp
from jax import lax
from jax.sharding import PartitionSpec as P

SUBITERS = 2
KRYLOV = 2


exact_mode = lax.Precision.HIGHEST


def extended(value, sides, width, wrap):
    for axis, dim in sides:
        size, length = (lax.axis_size(axis), value.shape[dim])
        up = [(i, (i + 1) % size) for i in range(size if wrap else size - 1)]
        down = [(j, i) for i, j in up]
        last = lax.slice_in_dim(value, length - width, length, axis=dim)
        initial = lax.slice_in_dim(value, 0, width, axis=dim)
        before = lax.ppermute(last, axis, up)
        after = lax.ppermute(initial, axis, down)
        value = jnp.concatenate([before, value, after], axis=dim)
    return value


def node_product(matrix, field):
    flat = field.reshape(field.shape[0], -1)
    return jnp.dot(matrix, flat, precision=exact_mode).reshape(field.shape)


def span_neighbours(field):
    padded = extended(field, (("span", 1),), 1, True)
    return (padded[:, :-2, :], padded[:, 2:, :])


def operate(field, coefficient, mats):
    volume_matrix, span_lower, span_upper, cross_lower, cross_upper = mats
    below, above = span_neighbours(field)
    padded = extended(field, (("xs", 2),), 1, False)
    left = padded[:, :, :-2]
    right = padded[:, :, 2:]
    result = coefficient * field + node_product(volume_matrix, field)
    result = result - node_product(span_lower, below) - node_product(span_upper, above)
    return result - node_product(cross_lower, left) - node_product(cross_upper, right)


def gmres(rhs, coefficient, mats):
    start_norm = jnp.sqrt(lax.psum(jnp.sum(rhs * rhs), ("span", "xs")))
    basis = [(rhs / start_norm).reshape(-1)]
    columns = []
    for step in range(KRYLOV):
        image = operate(basis[-1].reshape(rhs.shape), coefficient, mats).reshape(-1)
        stacked = jnp.stack(basis)
        project = lax.psum(jnp.dot(stacked, image, precision=exact_mode), ("span", "xs"))
        image = image - jnp.dot(project, stacked, precision=exact_mode)
        length = jnp.sqrt(lax.psum(jnp.sum(image * image), ("span", "xs")))
        columns.append(
            jnp.concatenate([project, length[None], jnp.zeros((KRYLOV - step - 1,), jnp.float32)])
        )
        basis.append(image / length)
    hessen = jnp.stack(columns, axis=1)
    gram = jnp.dot(hessen.T, hessen, precision=exact_mode)
    target = start_norm * hessen[0]
    factor = jnp.linalg.cholesky(gram)
    coeffs = jax.scipy.linalg.cho_solve((factor, True), target)
    result = jnp.dot(coeffs, jnp.stack(basis[:KRYLOV]), precision=exact_mode)
    return result.reshape(rhs.shape)


def shell_response(fluid, interface, compliance):
    indices = interface[0, 0]
    traces = fluid.reshape(-1)[indices]
    rows = compliance[0]
    empty = jnp.zeros((rows.shape[0],), jnp.float32)
    return empty + jnp.dot(
        rows, lax.all_gather(traces, "xs", axis=0, tiled=True), precision=exact_mode
    )


def body(
    source,
    coefficient,
    volume_matrix,
    span_lower,
    span_upper,
    cross_lower,
    cross_upper,
    interface,
    compliance,
    start_displacement,
):
    mats = (volume_matrix, span_lower, span_upper, cross_lower, cross_upper)
    displacement = start_displacement[0, 0]
    indices = interface[0, 0]
    fluid = source
    for sub in range(SUBITERS):
        forcing = jnp.zeros((source.size,), jnp.float32).at[indices].add(displacement)
        rhs = source + forcing.reshape(source.shape)
        fluid = gmres(rhs, coefficient, mats)
        fresh = shell_response(fluid, interface, compliance)
        displacement = 0.5 * fresh + 0.5 * displacement
    return (fluid, displacement[None, None, :])


def solution(mesh):
    placed = (
        P(None, "span", "xs"),
        P(None, "span", "xs"),
        P(),
        P(),
        P(),
        P(),
        P(),
        P("span", "xs", None),
        P("span", "xs", None),
        P("span", "xs", None),
    )
    return jax.shard_map(
        body,
        mesh=mesh,
        in_specs=placed,
        out_specs=(P(None, "span", "xs"), P("span", "xs", None)),
        check_vma=False,
    )
```

profile of v0, /device:TPU:1, one launch (start us, length us, event | category | flops | bytes accessed | tf_op | source)
XLA Modules:
  0.0 829.8 jit_solution(5862873896150614335)
XLA Ops:
  2.0 1.4 scatter_custom_fusion
  5.2 68.7 %psum.70 = f32[]{:T(128)} all-reduce(f32[]{:T(128)} %get-tuple-element.10), channel_id=1, replica_groups=mesh['span'=8,'xs'=16] {'span','xs'}, use_global_device_ids=true, to_apply=%region_2.0 | all-reduce | flops 1 | bytes 8 | tf_op jit(solution)/shard_map/psum | solution.py:48
  74.8 2.0 collective-permute-start.2
  76.8 1.3 collective-permute-start.3
  78.2 1.0 collective-permute-start
  80.8 0.9 collective-permute-done.2
  81.7 3.8 collective-permute-done.3
  94.0 66.7 %psum.71 = f32[1]{0:T(128)} all-reduce(f32[1]{0:T(128)} %bitcast.8), channel_id=1, replica_groups=mesh['span'=8,'xs'=16] {'span','xs'}, use_global_device_ids=true, to_apply=%region_3.0 | all-reduce | flops 1 | bytes 8 | tf_op jit(solution)/shard_map/psum | solution.py:54
  160.7 1.4 multiply_reduce_fusion.6
  162.1 1.3 stack_reshape.4
  163.4 62.9 %psum.72 = f32[]{:T(128)} all-reduce(f32[]{:T(128)} %multiply_reduce_fusion.6), channel_id=1, replica_groups=mesh['span'=8,'xs'=16] {'span','xs'}, use_global_device_ids=true, to_apply=%region_5.0 | all-reduce | flops 1 | bytes 8 | tf_op jit(solution)/shard_map/psum | solution.py:56
  229.3 2.4 collective-permute-start.6
  231.7 1.5 collective-permute-start.7
  235.3 1.3 stack.35
  236.8 3.7 collective-permute-done.7
  245.2 1.3 reshape.298
  246.5 10.6 %convolution_bitcast_fusion.3 = f32[2]{0:T(128)S(1)} fusion(f32[131072,1]{0,1:T(1,128)} %reshape.298, f32[1,131072]{1,0:T(1,128)S(1)} %copy-done.11, f32[1,131072]{1,0:T(1,128)S(1)} %copy-done.9), kind=kOutput, calls=%fused_computation.7 | convolution fusion | flops 3407872 | bytes 1572872 | tf_op jit(solution)/shard_map/dot_general | solution.py:54
  257.1 66.7 %psum.73 = f32[2]{0:T(128)S(1)} all-reduce(f32[2]{0:T(128)S(1)} %convolution_bitcast_fusion.3), channel_id=1, replica_groups=mesh['span'=8,'xs'=16] {'span','xs'}, use_global_device_ids=true, to_apply=%region_6.0 | all-reduce | flops 2 | bytes 16 | tf_op jit(solution)/shard_map/psum | solution.py:54
  323.8 4.1 fusion.29
  329.6 64.1 %psum.74 = f32[]{:T(128)} all-reduce(f32[]{:T(128)} %multiply_reduce_fusion.5), channel_id=1, replica_groups=mesh['span'=8,'xs'=16] {'span','xs'}, use_global_device_ids=true, to_apply=%region_8.0 | all-reduce | flops 1 | bytes 8 | tf_op jit(solution)/shard_map/psum | solution.py:56
  396.9 4.1 fusion.32
  401.0 1.1 gather_fusion
  402.2 13.9 %all-gather.2 = f32[16,1,128]{2,1,0:T(1,128)S(1)} all-gather(f32[1,1,128]{2,1,0:T(1,128)S(1)} %bitcast.401), channel_id=2, replica_groups=mesh['span'=8,'xs'=16] {'xs'}, dimensions={0}, use_global_device_ids=true | all-gather | bytes 8704 | tf_op jit(solution)/shard_map/all_gather | solution.py:76
  417.0 1.4 scatter_custom_fusion.1
  420.2 66.4 %psum.75 = f32[]{:T(128)} all-reduce(f32[]{:T(128)} %get-tuple-element.6), channel_id=1, replica_groups=mesh['span'=8,'xs'=16] {'span','xs'}, use_global_device_ids=true, to_apply=%region_13.0 | all-reduce | flops 1 | bytes 8 | tf_op jit(solution)/shard_map/psum | solution.py:48
  487.6 3.5 collective-permute-start.10
  491.1 1.5 collective-permute-start.11
  492.6 1.2 collective-permute-start.9
  494.8 1.0 collective-permute-done.10
  495.7 3.8 collective-permute-done.11
  504.8 66.2 %psum.76 = f32[1]{0:T(128)} all-reduce(f32[1]{0:T(128)} %bitcast.40), channel_id=1, replica_groups=mesh['span'=8,'xs'=16] {'span','xs'}, use_global_device_ids=true, to_apply=%region_14.0 | all-reduce | flops 1 | bytes 8 | tf_op jit(solution)/shard_map/psum | solution.py:54
  571.1 1.4 multiply_reduce_fusion.3
  572.4 1.3 stack_reshape.5
  573.8 64.0 %psum.77 = f32[]{:T(128)} all-reduce(f32[]{:T(128)} %multiply_reduce_fusion.3), channel_id=1, replica_groups=mesh['span'=8,'xs'=16] {'span','xs'}, use_global_device_ids=true, to_apply=%region_16.0 | all-reduce | flops 1 | bytes 8 | tf_op jit(solution)/shard_map/psum | solution.py:56
  640.7 2.0 collective-permute-start.14
  642.7 1.5 collective-permute-start.15
  644.2 1.7 collective-permute-start.12
  647.4 4.2 collective-permute-done.15
  651.7 1.5 pad_maximum_fusion.5
  658.4 9.4 %convolution_bitcast_fusion.1 = f32[2]{0:T(128)S(1)} fusion(f32[131072,1]{0,1:T(1,128)S(1)} %reshape.313, f32[1,131072]{1,0:T(1,128)S(1)} %stack.40, f32[1,131072]{1,0:T(1,128)S(1)} %copy-done.10), kind=kOutput, calls=%fused_computation.5 | convolution fusion | flops 3407872 | bytes 1572872 | tf_op jit(solution)/shard_map/dot_general | solution.py:54
  667.8 66.9 %psum.78 = f32[2]{0:T(128)S(1)} all-reduce(f32[2]{0:T(128)S(1)} %convolution_bitcast_fusion.1), channel_id=1, replica_groups=mesh['span'=8,'xs'=16] {'span','xs'}, use_global_device_ids=true, to_apply=%region_17.0 | all-reduce | flops 2 | bytes 16 | tf_op jit(solution)/shard_map/psum | solution.py:54
  734.6 4.1 fusion.27
  740.5 62.6 %psum.79 = f32[]{:T(128)} all-reduce(f32[]{:T(128)} %multiply_reduce_fusion.2), channel_id=1, replica_groups=mesh['span'=8,'xs'=16] {'span','xs'}, use_global_device_ids=true, to_apply=%region_19.22 | all-reduce | flops 1 | bytes 8 | tf_op jit(solution)/shard_map/psum | solution.py:56
  806.1 4.1 fusion.31
  810.3 1.1 gather_fusion.1
  811.4 0.9 reshape.256
  812.4 15.5 %all-gather.3 = f32[16,1,128]{2,1,0:T(1,128)S(1)} all-gather(f32[1,1,128]{2,1,0:T(1,128)S(1)} %bitcast.400), channel_id=3, replica_groups=mesh['span'=8,'xs'=16] {'xs'}, dimensions={0}, use_global_device_ids=true | all-gather | bytes 8704 | tf_op jit(solution)/shard_map/all_gather | solution.py:76
  827.9 1.4 fusion.3
  (163 shorter events, 48.5 us)
Async XLA Ops:
  0.6 415.4 %copy-start = (f32[1,128,2048]{2,1,0:T(8,128)S(1)}, f32[1,128,2048]{2,1,0:T(8,128)}, u32[]{:S(2)}) copy-start(f32[1,128,2048]{2,1,0:T(8,128)} %param.21) | copy-start | bytes 3145732
  1.4 0.7 copy-start.13
  3.4 1.0 copy-start.2
  74.8 6.9 collective-permute-start.2
  76.8 8.8 %collective-permute-start.3 = (f32[64,8,1]{2,1,0:T(8,128)S(1)}, f32[64,8,1]{2,1,0:T(8,128)S(1)}, u32[]{:S(2)}, u32[]{:S(2)}) collective-permute-start(f32[64,8,1]{2,1,0:T(8,128)S(1)} %get-tuple-element.43), channel_id=1, source_target_pairs={{1,0},{2,1},{3,2},{4,3},{5,4},{6,5},{7,6},{8,7},{9,8},{10,9},{11,1... | collective-permute-start | bytes 6152 | tf_op jit(solution)/shard_map/ppermute | solution.py:21
  78.2 7.4 collective-permute-start
  79.2 6.4 collective-permute-start.1
  79.2 0.8 copy-start.4
  86.1 0.8 copy-start.5
  87.6 0.8 copy-start.6
  89.2 0.8 copy-start.7
  90.7 0.8 copy-start.8
  92.1 1.0 copy-start.1
  229.3 7.5 collective-permute-start.6
  231.7 8.8 %collective-permute-start.7 = (f32[64,8,1]{2,1,0:T(8,128)}, f32[64,8,1]{2,1,0:T(8,128)S(1)}, u32[]{:S(2)}, u32[]{:S(2)}) collective-permute-start(f32[64,8,1]{2,1,0:T(8,128)} %get-tuple-element.35), channel_id=1, source_target_pairs={{1,0},{2,1},{3,2},{4,3},{5,4},{6,5},{7,6},{8,7},{9,8},{10,9},{11,1... | collective-permute-start | bytes 6152 | tf_op jit(solution)/shard_map/ppermute | solution.py:21
  233.2 7.3 collective-permute-start.4
  233.8 6.7 collective-permute-start.5
  245.1 1.3 copy-start.9
  245.2 1.3 copy-start.11
  328.2 68.7 %copy-start.12 = (f32[1,131072]{1,0:T(1,128)S(1)}, f32[1,131072]{1,0:T(1,128)}, u32[]{:S(2)}) copy-start(f32[1,131072]{1,0:T(1,128)} %stack.35) | copy-start | bytes 1572868
  418.4 1.0 copy-start.3
  487.6 8.2 collective-permute-start.10
  491.1 8.5 %collective-permute-start.11 = (f32[64,8,1]{2,1,0:T(8,128)S(1)}, f32[64,8,1]{2,1,0:T(8,128)S(1)}, u32[]{:S(2)}, u32[]{:S(2)}) collective-permute-start(f32[64,8,1]{2,1,0:T(8,128)S(1)} %get-tuple-element.27), channel_id=1, source_target_pairs={{1,0},{2,1},{3,2},{4,3},{5,4},{6,5},{7,6},{8,7},{9,8},{10,9},{11,1... | collective-permute-start | bytes 6152 | tf_op jit(solution)/shard_map/ppermute | solution.py:21
  492.5 7.1 collective-permute-start.8
  492.6 7.0 collective-permute-start.9
  640.7 6.7 collective-permute-start.14
  642.7 8.9 %collective-permute-start.15 = (f32[64,8,1]{2,1,0:T(8,128)}, f32[64,8,1]{2,1,0:T(8,128)}, u32[]{:S(2)}, u32[]{:S(2)}) collective-permute-start(f32[64,8,1]{2,1,0:T(8,128)} %get-tuple-element.19), channel_id=1, source_target_pairs={{1,0},{2,1},{3,2},{4,3},{5,4},{6,5},{7,6},{8,7},{9,8},{10,9},{11,1... | collective-permute-start | bytes 6152 | tf_op jit(solution)/shard_map/ppermute | solution.py:21
  644.2 7.4 collective-permute-start.12
  645.9 5.8 collective-permute-start.13
  657.3 1.0 copy-start.10
where the time goes:
time: 844 us; the launch traced here: 830 us
  blocking collectives  685 us (81%)
  matrix products  51.8 us (6%)
  local copies, waits for them, and re-layouts  27.4 us (3%)
  other arithmetic  21.5 us (3%)
  starting transfers between devices  20.9 us (2%)
  waiting for transfers between devices  17.6 us (2%)
    psum x4, blocking collectives, gmres(): lax.psum(jnp.dot(stacked, image, precision=exact_mode), ('span', 'xs'))  266 us
    psum x4, blocking collectives, gmres(): length = jnp.sqrt(lax.psum(jnp.sum(image * image), ('span', 'xs')))  254 us
    psum x2, blocking collectives, gmres(): start_norm = jnp.sqrt(lax.psum(jnp.sum(rhs * rhs), ('span', 'xs')))  135 us
    all_gather x2, blocking collectives, shell_response(): lax.all_gather(traces, 'xs', axis=0, tiled=True)  29.4 us
    dot_general x2, matrix products, gmres(): jnp.dot(stacked, image, precision=exact_mode)  19.9 us
  transfers between devices with their start and end apart: 16, of which 6 were waited for; matrix products, arithmetic and copies ran while one was open for 1% of the time, Pallas kernels for 0%

commit v1 on v0

v1 whole, which is shorter than its diff:
```python
import jax
import jax.numpy as jnp
from jax import lax
from jax.experimental import pallas as pl
from jax.experimental.pallas import tpu as pltpu
from jax.sharding import PartitionSpec as P

NODES, ES, EX, IFN = 64, 8, 256, 128
LANES = EX + 128
AXES = ("span", "xs")
THETA = 3.75
f32 = jnp.float32
bf16 = jnp.bfloat16
NT = (((1,), (1,)), ((), ()))


def parts(x):
    hi = x.astype(bf16)
    return hi, (x - hi.astype(f32)).astype(bf16)


def place(i):
    i = i.astype(jnp.int32)
    return i >> 11, (i >> 8) & 7, i & 255


def onehot(pos, size):
    rows = lax.broadcasted_iota(jnp.int32, (size, IFN), 0)
    return rows == pos


def pick(mask):
    return jnp.where(mask, 1.0, 0.0).astype(bf16)


def lane_rows(entries):
    rows = lax.broadcasted_iota(jnp.int32, (128, 128), 0)
    tile = jnp.zeros((128, 128), f32)
    for pos, value in entries:
        tile = jnp.where(rows == pos, value, tile)
    return tile.T


def fluid_kernel(
    src, cf, below, above, left, right, own, dmid, dbel, dabv, mats, mask,
    msg, *rest,
):
    *kept, r_scr, v_scr, l_scr = rest
    i_mid = (left[12:13], own[0:1], right[12:13])
    i_bel = (below[192:193, 128:], below[193:194, :128], below[193:194, 128:])
    i_abv = (above[192:193, 128:], above[193:194, :128], above[193:194, 128:])

    def forcing(idx, disp, shift, size):
        spots = [place(i) for i in idx]
        rows = [onehot((s + shift) * NODES + n, size) for n, s, _ in spots]
        d = [disp[k : k + 1] for k in range(3)]
        x = spots[1][2]
        sel = pick(rows[1])
        cols = parts(jnp.where(onehot(x, EX), d[1], 0.0))
        body = lax.dot_general(
            jnp.concatenate([sel, sel], 1), jnp.concatenate(cols, 1), NT,
            preferred_element_type=f32,
        )
        xl, xr = spots[0][2], spots[2][2]
        cl = parts(jnp.where(onehot(jnp.where(xl >= EX - 2, xl - 128, -1), 128), d[0], 0.0))
        cr = parts(jnp.where(onehot(jnp.where(xr < 2, xr, -1), 128), d[2], 0.0))
        sl, sr = pick(rows[0]), pick(rows[2])
        side = lax.dot_general(
            jnp.concatenate([sl, sl, sr, sr], 1), jnp.concatenate(cl + cr, 1), NT,
            preferred_element_type=f32,
        )
        return body, side, rows[1], x

    body, side, row_mask, x_own = forcing(i_mid, dmid, 0, ES * NODES)
    for s in range(ES):
        at = slice((s + 2) * NODES, (s + 3) * NODES)
        r_scr[at, :EX] = src[s * NODES : (s + 1) * NODES, :] + body[s * NODES : (s + 1) * NODES]
    for p in range(4):
        at = slice((2 * p + 2) * NODES, (2 * p + 4) * NODES)
        tile = lane_rows(
            ((0, right[p : p + 1]), (1, right[4 + p : 5 + p]), (126, left[p : p + 1]), (127, left[4 + p : 5 + p]))
        )
        r_scr[at, EX:] = tile + side[2 * p * NODES : (2 * p + 2) * NODES]
        l_scr[at, :] = lane_rows(((0, right[8 + p : 9 + p]), (127, left[8 + p : 9 + p])))
    cb, ct = below[192:193, :128], above[192:193, :128]
    half = lax.broadcasted_iota(jnp.int32, (1, 128), 1) < NODES
    corner = lane_rows(
        (
            (0, jnp.where(half, pltpu.roll(cb, NODES, 1), ct)),
            (127, jnp.where(half, cb, pltpu.roll(ct, NODES, 1))),
        )
    )
    body, side, _, _ = forcing(i_bel, dbel, 2 - ES, 2 * NODES)
    r_scr[: 2 * NODES, :EX] = below[: 2 * NODES] + body
    r_scr[: 2 * NODES, EX:] = side
    r_scr[NODES : 2 * NODES, EX:] += corner[:NODES]
    body, side, _, _ = forcing(i_abv, dabv, 0, 2 * NODES)
    r_scr[10 * NODES :, :EX] = above[: 2 * NODES] + body
    r_scr[10 * NODES :, EX:] = side
    r_scr[10 * NODES : 11 * NODES, EX:] += corner[NODES:]

    def product(ref, s, lo, hi):
        x = ref[s * NODES : (s + 1) * NODES, :]
        xh, xl = parts(x)
        return jnp.dot(
            mats[lo * NODES : hi * NODES, :], jnp.concatenate([xh, xh, xl], 0),
            preferred_element_type=f32,
        )

    def base(prod):
        return (
            prod[:NODES]
            + pltpu.roll(prod[3 * NODES : 4 * NODES], 1, 1)
            + pltpu.roll(prod[4 * NODES :], LANES - 1, 1)
        )

    def coef(s):
        if s == 1:
            return jnp.concatenate([below[2 * NODES : 3 * NODES], jnp.zeros((NODES, 128), f32)], 1)
        if s == 10:
            return jnp.concatenate([above[2 * NODES : 3 * NODES], jnp.zeros((NODES, 128), f32)], 1)
        return jnp.concatenate(
            [cf[(s - 2) * NODES : (s - 1) * NODES, :], l_scr[s * NODES : (s + 1) * NODES, :]], 1
        )

    keep = mask[0:1, :]
    low = product(r_scr, 0, 1, 2)
    pending = None
    for s in range(1, 12):
        if s < 11:
            prod = product(r_scr, s, 0, 5)
            up = prod[2 * NODES : 3 * NODES]
        else:
            up = product(r_scr, s, 2, 3)
        if pending is not None:
            v_scr[(s - 1) * NODES : s * NODES, :] = (pending + up) * keep
        if s < 11:
            pending = coef(s) * r_scr[s * NODES : (s + 1) * NODES, :] + base(prod) + low
            low = prod[NODES : 2 * NODES]

    sums = [jnp.zeros((8, EX), f32) for _ in range(5)]
    low = product(v_scr, 1, 1, 2)[:, :EX]
    pending = None
    for s in range(2, 11):
        if s < 10:
            prod = product(v_scr, s, 0, 5)
            up = prod[2 * NODES : 3 * NODES, :EX]
        else:
            up = product(v_scr, s, 2, 3)[:, :EX]
        if pending is not None:
            at = slice((s - 1) * NODES, s * NODES)
            r, v = r_scr[at, :EX], v_scr[at, :EX]
            w = pending + up - THETA * v
            pairs = ((v, v), (v, w), (w, w), (r, v), (r, w))
            for k, (a, b) in enumerate(pairs):
                sums[k] = sums[k] + jnp.sum((a * b).reshape(8, 8, EX), axis=0)
        if s < 10:
            at = slice(s * NODES, (s + 1) * NODES)
            pending = cf[(s - 2) * NODES : (s - 1) * NODES, :] * v_scr[at, :EX] + base(prod)[:, :EX] + low
            low = prod[NODES : 2 * NODES, :EX]

    lane = lax.broadcasted_iota(jnp.int32, (1, 128), 1)
    gram = jnp.zeros((1, 128), f32)
    for k in range(5):
        total = jnp.sum(jnp.sum(sums[k], axis=0, keepdims=True), axis=1, keepdims=True)
        gram = gram + jnp.where(lane == k, total, 0.0)
    cols = pick(onehot(x_own, EX))
    cols = jnp.concatenate([cols, cols], 0)
    rows = [gram]
    for ref in (r_scr, v_scr):
        hi, lo = parts(ref[2 * NODES : 10 * NODES, :EX])
        found = jnp.dot(jnp.concatenate([hi, lo], 1), cols, preferred_element_type=f32)
        rows.append(jnp.sum(jnp.where(row_mask, found, 0.0), axis=0, keepdims=True))
    msg[...] = jnp.broadcast_to(jnp.concatenate(rows, 1), msg.shape)
    if kept:
        kept[0][...] = r_scr[2 * NODES : 10 * NODES, :EX]
        kept[1][...] = v_scr[2 * NODES : 10 * NODES, :EX]


def solve(got):
    total = jnp.sum(got[:, :128], axis=0, keepdims=True)
    lane = lax.broadcasted_iota(jnp.int32, (1, 128), 1)
    g11, g12, g22, g1, g2 = (
        jnp.sum(jnp.where(lane == k, total, 0.0), axis=1, keepdims=True) for k in range(5)
    )
    ratio = g12 / g11
    b = (g2 - ratio * g1) / (g22 - ratio * g12)
    a = (g1 - b * g12) / g11
    return a - THETA * b, b


def shell_kernel(section, got, compliance, disp, *rest):
    if len(rest) > 1:
        r, v, fluid, out = rest
    else:
        (out,) = rest
    a, b = solve(got)
    start = pl.multiple_of(section[0] * 16, 16)
    traces = a * got[pl.ds(start, 16), 128:256] + b * got[pl.ds(start, 16), 256:]
    acc = jnp.zeros((IFN, 128), f32)
    for j in range(16):
        acc = acc + compliance[:, j * 128 : (j + 1) * 128] * traces[j : j + 1]
    fresh = jnp.sum(acc.T, axis=0, keepdims=True)
    out[...] = 0.5 * fresh + 0.5 * disp[0:1]
    if len(rest) > 1:
        for s in range(ES):
            at = slice(s * NODES, (s + 1) * NODES)
            fluid[:, s, :] = a * r[at, :] + b * v[at, :]


def columns(field, lo, hi):
    return jnp.transpose(field[:, :, lo:hi], (2, 1, 0)).reshape(-1, 128)


def layers(field, lo, hi):
    return jnp.transpose(field[:, lo:hi, :], (1, 0, 2)).reshape(-1, EX)


def body(
    source, coefficient, volume_matrix, span_lower, span_upper, cross_lower,
    cross_upper, interface, compliance, start_displacement,
):
    n_span, n_xs = lax.axis_size("span"), lax.axis_size("xs")
    up = [(i, i + 1) for i in range(n_xs - 1)]
    down = [(i + 1, i) for i in range(n_xs - 1)]
    fore = [(i, (i + 1) % n_span) for i in range(n_span)]
    back = [((i + 1) % n_span, i) for i in range(n_span)]
    disp = start_displacement[0]
    own = interface[0].astype(f32)
    tail = [own, disp, jnp.zeros((2, 128), f32)]
    left = lax.ppermute(
        jnp.concatenate([columns(source, EX - 2, EX), columns(coefficient, EX - 1, EX)] + tail), "xs", up
    )
    right = lax.ppermute(
        jnp.concatenate([columns(source, 0, 2), columns(coefficient, 0, 1)] + tail), "xs", down
    )
    stacked = jnp.concatenate(
        [volume_matrix, -span_lower, -span_upper, -cross_lower, -cross_upper], 0
    )
    high = lax.reduce_precision(stacked, 8, 7)
    mats = jnp.concatenate([high, stacked - high, high], 1).astype(bf16)
    index = lax.axis_index("xs")
    lane = jnp.arange(LANES)
    inside = (lane < EX) | ((lane < EX + 2) & (index < n_xs - 1)) | ((lane >= LANES - 2) & (index > 0))
    mask = jnp.broadcast_to(jnp.where(inside, 1.0, 0.0).astype(f32)[None], (8, LANES))
    section = lax.axis_index("span").astype(jnp.int32)[None]

    def edge(first, corner_l, corner_r):
        corner = jnp.concatenate([corner_l, corner_r])[None]
        small = jnp.concatenate(
            [corner, left[12:13], own, right[12:13], left[13:14], disp, right[13:14]]
            + [jnp.zeros((9, 128), f32)]
        ).reshape(8, EX)
        inner = ES - 1 if first else 0
        both = layers(source, ES - 2, ES) if first else layers(source, 0, 2)
        return jnp.concatenate([both, layers(coefficient, inner, inner + 1), small])

    below = lax.ppermute(edge(True, left[7, NODES:], right[3, NODES:]), "span", fore)
    above = lax.ppermute(edge(False, left[4, :NODES], right[0, :NODES]), "span", back)

    src = layers(source, 0, ES)
    cf = layers(coefficient, 0, ES)

    def tails(edges):
        return edges[194:196].reshape(4, 128)[:3]

    def fluid_step(dmid, dbel, dabv, keep):
        shapes = [jax.ShapeDtypeStruct((128, 3 * 128), f32)]
        if keep:
            shapes += [jax.ShapeDtypeStruct((ES * NODES, EX), f32)] * 2
        return pl.pallas_call(
            fluid_kernel,
            out_shape=shapes,
            scratch_shapes=[
                pltpu.VMEM((12 * NODES, LANES), f32),
                pltpu.VMEM((12 * NODES, LANES), f32),
                pltpu.VMEM((12 * NODES, 128), f32),
            ],
            name="fluid_keep" if keep else "fluid",
        )(src, cf, below, above, left, right, own, dmid, dbel, dabv, mats, mask)

    vm = pl.BlockSpec(memory_space=pltpu.VMEM)
    sm = pl.BlockSpec(memory_space=pltpu.SMEM)

    def exchange(message):
        return lax.all_to_all(message, AXES, 0, 0)

    rows = compliance[0]
    dmid = jnp.concatenate([left[13:14], disp, right[13:14]])
    (message,) = fluid_step(dmid, tails(below), tails(above), False)
    got = exchange(message)
    disp = pl.pallas_call(
        shell_kernel,
        out_shape=jax.ShapeDtypeStruct((1, 128), f32),
        in_specs=[sm, vm, vm, vm],
        out_specs=vm,
        name="shell",
    )(section, got, rows, disp)
    dl = lax.ppermute(disp, "xs", up)
    dr = lax.ppermute(disp, "xs", down)
    dmid = jnp.concatenate([dl, disp, dr])
    dbel = lax.ppermute(dmid, "span", fore)
    dabv = lax.ppermute(dmid, "span", back)
    message, r, v = fluid_step(dmid, dbel, dabv, True)
    got = exchange(message)
    fluid, disp = pl.pallas_call(
        shell_kernel,
        out_shape=[
            jax.ShapeDtypeStruct((NODES, ES, EX), f32),
            jax.ShapeDtypeStruct((1, 128), f32),
        ],
        in_specs=[sm, vm, vm, vm, vm, vm],
        out_specs=[vm, vm],
        name="shell_last",
    )(section, got, rows, disp, r, v)
    return fluid, disp[None]


def solution(mesh):
    field = P(None, "span", "xs")
    section = P("span", "xs", None)
    return jax.shard_map(
        body,
        mesh=mesh,
        in_specs=(field, field, P(), P(), P(), P(), P(), section, section, section),
        out_specs=(field, section),
        check_vma=False,
    )
```

time: 844 us -> 98 us (0.12); the launches traced: 830 us -> 97.2 us
  blocking collectives: 685 us -> 18.6 us
  matrix products: 51.8 us -> 0 us
  other arithmetic: 21.5 us -> 2.88 us
  Pallas kernels: 0 us -> 14.2 us
  local copies, waits for them, and re-layouts: 27.4 us -> 16.7 us
    psum x10 -> x0, blocking collectives: 655 us -> none  [the longest x4 266 us: gmres(): lax.psum(jnp.dot(stacked, image, precision=exact_mode), ('span', 'xs'))]
    dot_general x30 -> x0, matrix products: 51.2 us -> none  [the longest x2 19.9 us: gmres(): jnp.dot(stacked, image, precision=exact_mode)]
    all_gather x2 -> x0, blocking collectives: 29.4 us -> none  [shell_response(): lax.all_gather(traces, 'xs', axis=0, tiled=True)]
    all_to_all x0 -> x1, blocking collectives: none -> 18.6 us  [exchange(): return lax.all_to_all(message, AXES, 0, 0)]
    pallas_call x0 -> x4, Pallas kernels: none -> 14.2 us  [the longest x2 9.31 us: fluid_step(): pl.pallas_call(fluid_kernel, out_shape=shapes, scratch_shapes=[pltpu.VMEM...]
    ppermute x16 -> x8, waiting for transfers between devices: 17.6 us -> 4.96 us  [the longest x1 2.8 us: body(): lax.ppermute(edge(False, left[4, :NODES], right[0, :NODES]), 'span', back)]
    all_to_all x0 -> x1, starting transfers between devices: none -> 12.1 us  [exchange(): return lax.all_to_all(message, AXES, 0, 0)]
    all_to_all x0 -> x1, waiting for transfers between devices: none -> 10.6 us  [exchange(): return lax.all_to_all(message, AXES, 0, 0)]
  transfers between devices with their start and end apart: 16 -> 9, of which waited for: 6 -> 4; matrix products, arithmetic and copies ran while one was open for 1% -> 5% of each run, Pallas kernels for 0% -> 0%
where the time goes in v1:
time: 98 us; the launch traced here: 97.2 us
  starting transfers between devices  28.4 us (29%)
  blocking collectives  18.6 us (19%)
  local copies, waits for them, and re-layouts  16.7 us (17%)
  waiting for transfers between devices  15.5 us (16%)
  Pallas kernels  14.2 us (14%)
  other arithmetic  2.88 us (3%)
    all_to_all x1, blocking collectives, exchange(): return lax.all_to_all(message, AXES, 0, 0)  18.6 us
    all_to_all x1, starting transfers between devices, exchange(): return lax.all_to_all(message, AXES, 0, 0)  12.1 us
    all_to_all x1, waiting for transfers between devices, exchange(): return lax.all_to_all(message, AXES, 0, 0)  10.6 us
    pallas_call x2, Pallas kernels, fluid_step(): pl.pallas_call(fluid_kernel, out_shape=shapes, scratch_shapes=[pltpu.VMEM...  9.31 us
    unnamed x37, local copies, waits for them, and re-layouts  6.97 us
    ppermute x1, starting transfers between devices, body(): lax.ppermute(jnp.concatenate([columns(source, EX - 2, EX), columns(coeffi...  4.56 us
    ppermute x1, starting transfers between devices, body(): dl = lax.ppermute(disp, 'xs', up)  3.99 us
    all_to_all x2, local copies, waits for them, and re-layouts, exchange(): return lax.all_to_all(message, AXES, 0, 0)  2.95 us
  transfers between devices with their start and end apart: 9, of which 4 were waited for; matrix products, arithmetic and copies ran while one was open for 5% of the time, Pallas kernels for 0%

profile of v1, /device:TPU:1, one launch (start us, length us, event | category | flops | bytes accessed | tf_op | source)
XLA Modules:
  0.0 97.2 jit_solution(17729901379822462273)
XLA Ops:
  0.6 0.7 convert_bitcast_fusion.own
  1.3 1.2 %slice_bitcast_fusion.3 = (f32[2,8,64]{0,1,2:T(8,128)S(1)}, f32[2,8,64]{0,1,2:T(8,128)S(1)}) fusion(f32[64,8,256]{2,1,0:T(8,128)} %param.10), kind=kLoop, calls=%fused_computation.3 | loop fusion | bytes 16384 | tf_op jit(solution)/shard_map/transpose | solution.py:212
  2.5 0.1 copy.28
  2.7 0.1 slice_bitcast_fusion.2
  2.9 0.1 copy.29
  3.1 0.3 copy-done.12
  3.4 1.3 %collective-permute-start.1 = (f32[16,128]{1,0:T(8,128)S(1)}, f32[16,128]{1,0:T(8,128)S(1)}, u32[]{:S(2)}, u32[]{:S(2)}) collective-permute-start(f32[16,128]{1,0:T(8,128)S(1)} %concatenate.38), channel_id=1, source_target_pairs={{1,0},{2,1},{3,2},{4,3},{5,4},{6,5},{7,6},{8,7},{9,8},{10,9},{11,1... | collective-permute-start | bytes 24584 | tf_op jit(solution)/shard_map/ppermute | solution.py:234
  4.7 0.1 copy.26
  4.9 0.2 copy.27
  5.2 4.6 %collective-permute-start = (f32[16,128]{1,0:T(8,128)S(1)}, f32[16,128]{1,0:T(8,128)S(1)}, u32[]{:S(2)}, u32[]{:S(2)}) collective-permute-start(f32[16,128]{1,0:T(8,128)S(1)} %concatenate.37), channel_id=1, source_target_pairs={{0,1},{1,2},{2,3},{3,4},{4,5},{5,6},{6,7},{7,8},{8,9},{9,10},{10,1... | collective-permute-start | bytes 24584 | tf_op jit(solution)/shard_map/ppermute | solution.py:231
  10.0 0.7 copy-done.6
  10.6 0.8 copy-done.7
  11.4 0.8 copy-done.8
  12.2 0.8 copy-done.9
  12.9 0.8 copy-done.10
  13.7 0.8 pad_maximum_fusion.2.mats
  14.5 1.0 copy.23
  15.5 1.0 copy.22
  16.7 0.4 copy-done.4
  17.1 0.1 concatenate.43
  17.3 0.1 concatenate.40
  17.5 1.4 %collective-permute-start.3 = (f32[200,256]{1,0:T(8,128)S(1)}, f32[200,256]{1,0:T(8,128)S(1)}, u32[]{:S(2)}, u32[]{:S(2)}) collective-permute-start(f32[200,256]{1,0:T(8,128)S(1)} %pad_maximum_fusion.1), channel_id=1, source_target_pairs={{16,0},{32,16},{48,32},{64,48},{80,64},{96,80},{112,96},{0,112},{1... | collective-permute-start | bytes 614408 | tf_op jit(solution)/shard_map/ppermute | solution.py:259
  18.9 1.7 %collective-permute-start.2 = (f32[200,256]{1,0:T(8,128)S(1)}, f32[200,256]{1,0:T(8,128)S(1)}, u32[]{:S(2)}, u32[]{:S(2)}) collective-permute-start(f32[200,256]{1,0:T(8,128)S(1)} %pad_maximum_fusion), channel_id=1, source_target_pairs={{0,16},{16,32},{32,48},{48,64},{64,80},{80,96},{96,112},{112,0},{1... | collective-permute-start | bytes 614408 | tf_op jit(solution)/shard_map/ppermute | solution.py:258
  20.6 0.6 pad_maximum_fusion.3.dmid
  21.1 2.8 %collective-permute-done.3.above = f32[200,256]{1,0:T(8,128)S(1)} collective-permute-done((f32[200,256]{1,0:T(8,128)S(1)}, f32[200,256]{1,0:T(8,128)S(1)}, u32[]{:S(2)}, u32[]{:S(2)}) %collective-permute-start.3) | collective-permute-done | bytes 204832 | tf_op jit(solution)/shard_map/ppermute | solution.py:259
  23.9 0.7 reshape.81
  24.6 0.6 reshape.80
  25.3 0.6 broadcast_in_dim.35.mask
  25.9 4.7 %fluid.1 = f32[128,384]{1,0:T(8,128)} custom-call(f32[512,256]{1,0:T(8,128)} %bitcast.54, f32[512,256]{1,0:T(8,128)} %bitcast.52, f32[200,256]{1,0:T(8,128)} %copy-done.3, f32[200,256]{1,0:T(8,128)} %copy-done.2, f32[16,128]{1,0:T(8,128)} %copy-done.5, f32[16,128]{1,0:T(8,128)} %copy-done.4, f32[1,128]{1,0:T(1,128)} %copy-done.11, ...), custom_call_target="tpu_custom_call" | custom-call | tf_op jit(solution)/shard_map/fluid/pallas_call | solution.py:271
  30.5 1.8 %copy.32 = f32[128,1,384]{2,1,0:T(1,128)} copy(f32[128,1,384]{2,0,1:T(8,128)} %bitcast.61) | data formatting | bytes 393216 | tf_op jit(solution)/shard_map/all_to_all | solution.py:286
  32.4 12.1 %all-to-all-start = ((f32[128,1,384]{2,1,0:T(1,128)}), f32[128,1,384]{2,1,0:T(1,128)S(1)}, u32[]{:S(2)}, u32[]{:S(2)}) async-start(f32[128,1,384]{2,1,0:T(1,128)} %copy.32), calls=%async_computation | async-start | bytes 393216 | tf_op jit(solution)/shard_map/all_to_all | solution.py:286
  44.5 10.6 %all-to-all-done = f32[128,1,384]{2,1,0:T(1,128)S(1)} async-done(((f32[128,1,384]{2,1,0:T(1,128)}), f32[128,1,384]{2,1,0:T(1,128)S(1)}, u32[]{:S(2)}, u32[]{:S(2)}) %all-to-all-start) | async-done | bytes 196640 | tf_op jit(solution)/shard_map/all_to_all | solution.py:286
  55.1 0.7 copy.43
  55.8 2.1 %shell.1.disp = f32[1,128]{1,0:T(1,128)} custom-call(s32[1]{0:T(128)} %bitcast.section, f32[128,384]{1,0:T(8,128)} %bitcast.62, f32[128,2048]{1,0:T(8,128)} %bitcast.56, f32[1,128]{1,0:T(1,128)} %bitcast.68), custom_call_target="tpu_custom_call" | custom-call | tf_op jit(solution)/shard_map/shell/pallas_call | solution.py:292
  57.9 1.3 %collective-permute-start.5 = (f32[1,128]{1,0:T(1,128)}, f32[1,128]{1,0:T(1,128)S(1)}, u32[]{:S(2)}, u32[]{:S(2)}) collective-permute-start(f32[1,128]{1,0:T(1,128)} %shell.1.disp), channel_id=1, source_target_pairs={{1,0},{2,1},{3,2},{4,3},{5,4},{6,5},{7,6},{8,7},{9,8},{10,9},{11,1... | collective-permute-start | bytes 1544 | tf_op jit(solution)/shard_map/ppermute | solution.py:300
  59.2 4.0 %collective-permute-start.4 = (f32[1,128]{1,0:T(1,128)}, f32[1,128]{1,0:T(1,128)S(1)}, u32[]{:S(2)}, u32[]{:S(2)}) collective-permute-start(f32[1,128]{1,0:T(1,128)} %shell.1.disp), channel_id=1, source_target_pairs={{0,1},{1,2},{2,3},{3,4},{4,5},{5,6},{6,7},{7,8},{8,9},{9,10},{10,1... | collective-permute-start | bytes 1544 | tf_op jit(solution)/shard_map/ppermute | solution.py:299
  63.2 0.9 collective-permute-done.4
  64.1 0.7 pad_maximum_fusion.4.dmid
  64.8 1.7 %collective-permute-start.7 = (f32[3,128]{1,0:T(4,128)S(1)}, f32[3,128]{1,0:T(4,128)S(1)}, u32[]{:S(2)}, u32[]{:S(2)}) collective-permute-start(f32[3,128]{1,0:T(4,128)S(1)} %pad_maximum_fusion.4.dmid), channel_id=1, source_target_pairs={{16,0},{32,16},{48,32},{64,48},{80,64},{96,80},{112,96},{0,112},{1... | collective-permute-start | bytes 4616 | tf_op jit(solution)/shard_map/ppermute | solution.py:303
  66.4 0.5 collective-permute-start.6
  66.9 1.2 %collective-permute-done.7.dabv = f32[3,128]{1,0:T(4,128)S(1)} collective-permute-done((f32[3,128]{1,0:T(4,128)S(1)}, f32[3,128]{1,0:T(4,128)S(1)}, u32[]{:S(2)}, u32[]{:S(2)}) %collective-permute-start.7) | collective-permute-done | bytes 1568 | tf_op jit(solution)/shard_map/ppermute | solution.py:303
  68.1 0.6 copy-done.14
  68.7 0.6 copy-done.15
  69.3 4.6 %fluid_keep.1 = (f32[128,384]{1,0:T(8,128)}, f32[512,256]{1,0:T(8,128)}, f32[512,256]{1,0:T(8,128)}) custom-call(f32[512,256]{1,0:T(8,128)} %bitcast.55, f32[512,256]{1,0:T(8,128)} %bitcast.53, f32[200,256]{1,0:T(8,128)} %copy-done.3, f32[200,256]{1,0:T(8,128)} %copy-done.2, f32[16,128]{1,0:T(8,128)} %copy-done.5, f32[16,128]{1,0:T(8,128)} %copy-done.4, ...), custom_call_target="tpu_custom_call" | custom-call | tf_op jit(solution)/shard_map/fluid_keep/pallas_call | solution.py:271
  73.9 1.1 %copy.33 = f32[128,1,384]{2,1,0:T(1,128)S(1)} copy(f32[128,1,384]{2,0,1:T(8,128)} %bitcast.67) | data formatting | bytes 393216 | tf_op jit(solution)/shard_map/all_to_all | solution.py:286
  75.1 18.6 %all_to_all.22 = f32[128,1,384]{2,1,0:T(1,128)S(1)} all-to-all(f32[128,1,384]{2,1,0:T(1,128)S(1)} %copy.33), channel_id=1, replica_groups=mesh['span'=8,'xs'=16] {'span','xs'}, dimensions={0} | all-to-all | bytes 393216 | tf_op jit(solution)/shard_map/all_to_all | solution.py:286
  93.7 0.7 copy.42
  94.4 2.8 %shell_last.1 = (f32[64,8,256]{2,1,0:T(8,128)}, f32[1,128]{1,0:T(1,128)}) custom-call(s32[1]{0:T(128)} %bitcast.section, f32[128,384]{1,0:T(8,128)} %bitcast.60, f32[128,2048]{1,0:T(8,128)} %bitcast.57, f32[1,128]{1,0:T(1,128)} %shell.1.disp, f32[512,256]{1,0:T(8,128)} %get-tuple-element.8.rest_0_, f32[512,256]{1,0:T(8,128)} %get-tuple-element.9.rest_1_), custom_call_target="tpu_custom_call" | custom-call | tf_op jit(solution)/shard_map/shell_last/pallas_call | solution.py:306
  (60 shorter events, 1.0 us)
Async XLA Ops:
  1.3 16.0 %copy-start.11 = (f32[1,128]{1,0:T(1,128)}, f32[1,128]{1,0:T(1,128)S(1)}, u32[]{:S(2)}) copy-start(f32[1,128]{1,0:T(1,128)S(1)} %convert_bitcast_fusion.own) | copy-start | bytes 1540
  1.3 1.4 %copy-start.1 = (f32[64,8,256]{2,1,0:T(8,128)S(1)}, f32[64,8,256]{2,1,0:T(8,128)}, u32[]{:S(2)}) copy-start(f32[64,8,256]{2,1,0:T(8,128)} %param.11) | copy-start | bytes 1572868
  2.7 0.7 copy-start.12
  2.9 7.0 %copy-start = (f32[64,8,256]{2,1,0:T(8,128)S(1)}, f32[64,8,256]{2,1,0:T(8,128)}, u32[]{:S(2)}) copy-start(f32[64,8,256]{2,1,0:T(8,128)} %param.10) | copy-start | bytes 1572868
  3.4 13.0 %collective-permute-start.1 = (f32[16,128]{1,0:T(8,128)S(1)}, f32[16,128]{1,0:T(8,128)S(1)}, u32[]{:S(2)}, u32[]{:S(2)}) collective-permute-start(f32[16,128]{1,0:T(8,128)S(1)} %concatenate.38), channel_id=1, source_target_pairs={{1,0},{2,1},{3,2},{4,3},{5,4},{6,5},{7,6},{8,7},{9,8},{10,9},{11,1... | collective-permute-start | bytes 24584 | tf_op jit(solution)/shard_map/ppermute | solution.py:234
  5.2 11.3 %collective-permute-start = (f32[16,128]{1,0:T(8,128)S(1)}, f32[16,128]{1,0:T(8,128)S(1)}, u32[]{:S(2)}, u32[]{:S(2)}) collective-permute-start(f32[16,128]{1,0:T(8,128)S(1)} %concatenate.37), channel_id=1, source_target_pairs={{0,1},{1,2},{2,3},{3,4},{4,5},{5,6},{6,7},{7,8},{8,9},{9,10},{10,1... | collective-permute-start | bytes 24584 | tf_op jit(solution)/shard_map/ppermute | solution.py:231
  9.9 0.8 copy-start.6
  10.6 0.8 copy-start.7
  11.4 0.8 copy-start.8
  12.2 0.8 copy-start.9
  12.9 0.8 copy-start.10
  16.5 0.6 copy-start.4
  16.5 0.6 copy-start.5
  17.5 6.5 %collective-permute-start.3 = (f32[200,256]{1,0:T(8,128)S(1)}, f32[200,256]{1,0:T(8,128)S(1)}, u32[]{:S(2)}, u32[]{:S(2)}) collective-permute-start(f32[200,256]{1,0:T(8,128)S(1)} %pad_maximum_fusion.1), channel_id=1, source_target_pairs={{16,0},{32,16},{48,32},{64,48},{80,64},{96,80},{112,96},{0,112},{1... | collective-permute-start | bytes 614408 | tf_op jit(solution)/shard_map/ppermute | solution.py:259
  18.9 5.7 %collective-permute-start.2 = (f32[200,256]{1,0:T(8,128)S(1)}, f32[200,256]{1,0:T(8,128)S(1)}, u32[]{:S(2)}, u32[]{:S(2)}) collective-permute-start(f32[200,256]{1,0:T(8,128)S(1)} %pad_maximum_fusion), channel_id=1, source_target_pairs={{0,16},{16,32},{32,48},{48,64},{64,80},{80,96},{96,112},{112,0},{1... | collective-permute-start | bytes 614408 | tf_op jit(solution)/shard_map/ppermute | solution.py:258
  23.9 1.9 %copy-start.2 = (f32[200,256]{1,0:T(8,128)}, f32[200,256]{1,0:T(8,128)S(1)}, u32[]{:S(2)}) copy-start(f32[200,256]{1,0:T(8,128)S(1)} %collective-permute-done.3.above) | copy-start | bytes 614404
  24.6 1.3 %copy-start.3 = (f32[200,256]{1,0:T(8,128)}, f32[200,256]{1,0:T(8,128)S(1)}, u32[]{:S(2)}) copy-start(f32[200,256]{1,0:T(8,128)S(1)} %collective-permute-done.2.below) | copy-start | bytes 614404
  32.4 22.7 %all-to-all-start = ((f32[128,1,384]{2,1,0:T(1,128)}), f32[128,1,384]{2,1,0:T(1,128)S(1)}, u32[]{:S(2)}, u32[]{:S(2)}) async-start(f32[128,1,384]{2,1,0:T(1,128)} %copy.32), calls=%async_computation | async-start | bytes 393216 | tf_op jit(solution)/shard_map/all_to_all | solution.py:286
  57.9 5.3 %collective-permute-start.5 = (f32[1,128]{1,0:T(1,128)}, f32[1,128]{1,0:T(1,128)S(1)}, u32[]{:S(2)}, u32[]{:S(2)}) collective-permute-start(f32[1,128]{1,0:T(1,128)} %shell.1.disp), channel_id=1, source_target_pairs={{1,0},{2,1},{3,2},{4,3},{5,4},{6,5},{7,6},{8,7},{9,8},{10,9},{11,1... | collective-permute-start | bytes 1544 | tf_op jit(solution)/shard_map/ppermute | solution.py:300
  59.2 4.9 %collective-permute-start.4 = (f32[1,128]{1,0:T(1,128)}, f32[1,128]{1,0:T(1,128)S(1)}, u32[]{:S(2)}, u32[]{:S(2)}) collective-permute-start(f32[1,128]{1,0:T(1,128)} %shell.1.disp), channel_id=1, source_target_pairs={{0,1},{1,2},{2,3},{3,4},{4,5},{5,6},{6,7},{7,8},{8,9},{9,10},{10,1... | collective-permute-start | bytes 1544 | tf_op jit(solution)/shard_map/ppermute | solution.py:299
  64.8 3.4 %copy-start.13 = (f32[3,128]{1,0:T(4,128)}, f32[3,128]{1,0:T(4,128)S(1)}, u32[]{:S(2)}) copy-start(f32[3,128]{1,0:T(4,128)S(1)} %pad_maximum_fusion.4.dmid) | copy-start | bytes 4612
  64.8 3.4 %collective-permute-start.7 = (f32[3,128]{1,0:T(4,128)S(1)}, f32[3,128]{1,0:T(4,128)S(1)}, u32[]{:S(2)}, u32[]{:S(2)}) collective-permute-start(f32[3,128]{1,0:T(4,128)S(1)} %pad_maximum_fusion.4.dmid), channel_id=1, source_target_pairs={{16,0},{32,16},{48,32},{64,48},{80,64},{96,80},{112,96},{0,112},{1... | collective-permute-start | bytes 4616 | tf_op jit(solution)/shard_map/ppermute | solution.py:303
  66.4 1.7 %collective-permute-start.6 = (f32[3,128]{1,0:T(4,128)S(1)}, f32[3,128]{1,0:T(4,128)S(1)}, u32[]{:S(2)}, u32[]{:S(2)}) collective-permute-start(f32[3,128]{1,0:T(4,128)S(1)} %pad_maximum_fusion.4.dmid), channel_id=1, source_target_pairs={{0,16},{16,32},{32,48},{48,64},{64,80},{80,96},{96,112},{112,0},{1... | collective-permute-start | bytes 4616 | tf_op jit(solution)/shard_map/ppermute | solution.py:302
  68.1 0.6 copy-start.14
  68.7 0.6 copy-start.15

commit v2 on v1

v2 whole, which is shorter than its diff:
```python
import jax
import jax.numpy as jnp
from jax import lax
from jax.experimental import pallas as pl
from jax.experimental.pallas import tpu as pltpu
from jax.sharding import PartitionSpec as P

NODES, ES, EX, IFN = 64, 8, 256, 128
LANES = EX + 128
AXES = ("span", "xs")
THETA = 3.75
f32 = jnp.float32
bf16 = jnp.bfloat16
NT = (((1,), (1,)), ((), ()))


def parts(x):
    hi = x.astype(bf16)
    return hi, (x - hi.astype(f32)).astype(bf16)


def place(i):
    i = i.astype(jnp.int32)
    return i >> 11, (i >> 8) & 7, i & 255


def onehot(pos, size):
    rows = lax.broadcasted_iota(jnp.int32, (size, IFN), 0)
    return rows == pos


def pick(mask):
    return jnp.where(mask, 1.0, 0.0).astype(bf16)


def lane_rows(entries):
    rows = lax.broadcasted_iota(jnp.int32, (128, 128), 0)
    tile = jnp.zeros((128, 128), f32)
    for pos, value in entries:
        tile = jnp.where(rows == pos, value, tile)
    return tile.T


def position():
    return lax.axis_index("span"), lax.axis_index("xs")


def pack_cross(src_hbm, cf_hbm, own_hbm, disp_hbm, first, second, own, disp, src, cf, scr, sems):
    pairs = ((src_hbm, src), (cf_hbm, cf), (own_hbm, own), (disp_hbm, disp))
    copies = [pltpu.make_async_copy(a, b, sems.at[k]) for k, (a, b) in enumerate(pairs)]
    for copy in copies:
        copy.start()
    for copy in copies:
        copy.wait()
    lane = lax.broadcasted_iota(jnp.int32, (2 * NODES, 128), 1)
    tile = jnp.zeros((2 * NODES, 128), f32)
    for p in range(4):
        for ref, wide, at in ((src, 2, 2 * p), (cf, 1, 8 + p)):
            both = jnp.concatenate([ref[:, 2 * p, :], ref[:, 2 * p + 1, :]], 0)
            high = pltpu.roll(both[:, 128:], at + wide, 1)
            low = pltpu.roll(both[:, :128], 64 + at, 1)
            tile = jnp.where((lane >= at) & (lane < at + wide), high, tile)
            tile = jnp.where((lane >= 64 + at) & (lane < 64 + at + wide), low, tile)
    scr[...] = tile.T
    odd = (position()[1] % 2) * 64
    for out, start in ((first, odd), (second, 64 - odd)):
        out[...] = scr[pl.ds(pl.multiple_of(start, 64), 16), :]
        out[12:13] = own[...].astype(f32)
        out[13:14] = disp[...]


def sides(index, first, second):
    even = index % 2 == 0
    return jnp.where(even, second, first), jnp.where(even, first, second)


def pack_span(src, cf, cross_a, cross_b, own, disp, first, second):
    where = position()
    half = lax.broadcasted_iota(jnp.int32, (1, 128), 1) < NODES
    mine = own[...].astype(f32)
    left, right = sides(where[1], cross_a[...], cross_b[...])
    even = where[0] % 2 == 0
    after = jnp.where(half, pltpu.roll(left[7:8], NODES, 1), right[6:7])
    before = jnp.where(half, left[1:2], pltpu.roll(right[0:1], NODES, 1))
    for out, top in ((first, even), (second, jnp.logical_not(even))):

        @pl.when(top)
        def _():
            out[:NODES] = src[:, ES - 2, :]
            out[NODES : 2 * NODES] = src[:, ES - 1, :]
            out[2 * NODES : 3 * NODES] = cf[:, ES - 1, :]

        @pl.when(jnp.logical_not(top))
        def _():
            out[:NODES] = src[:, 0, :]
            out[NODES : 2 * NODES] = src[:, 1, :]
            out[2 * NODES : 3 * NODES] = cf[:, 0, :]

        corner = jnp.where(top, after, before)
        out[192:193] = jnp.concatenate([corner, left[12:13]], 1)
        out[193:194] = jnp.concatenate([mine, right[12:13]], 1)
        out[194:195] = jnp.concatenate([left[13:14], disp[...]], 1)
        out[195:196] = jnp.concatenate([right[13:14], jnp.zeros((1, 128), f32)], 1)
        out[196:200] = jnp.zeros((4, EX), f32)


def join(cross_a, cross_b, d, out):
    dl, dr = sides(position()[1], cross_a[...], cross_b[...])
    out[...] = jnp.concatenate([dl, d[...], dr], 0)


def forcing(idx, disp, shift, size):
    spots = [place(i) for i in idx]
    rows = [onehot((s + shift) * NODES + n, size) for n, s, _ in spots]
    x = spots[1][2]
    sel = pick(rows[1])
    cols = parts(jnp.where(onehot(x, EX), disp[1], 0.0))
    main = lax.dot_general(
        jnp.concatenate([sel, sel], 1), jnp.concatenate(cols, 1), NT, preferred_element_type=f32
    )
    xl, xr = spots[0][2], spots[2][2]
    cl = parts(jnp.where(onehot(jnp.where(xl >= EX - 2, xl - 128, -1), 128), disp[0], 0.0))
    cr = parts(jnp.where(onehot(jnp.where(xr < 2, xr, -1), 128), disp[2], 0.0))
    sl, sr = pick(rows[0]), pick(rows[2])
    side = lax.dot_general(
        jnp.concatenate([sl, sl, sr, sr], 1), jnp.concatenate(cl + cr, 1), NT,
        preferred_element_type=f32,
    )
    return main, side, rows[1], x


def extend(src, cf, below, above, left, right, ext, edge):
    for s in range(ES):
        ext[(s + 2) * NODES : (s + 3) * NODES, :EX] = src[:, s, :]
    for p in range(4):
        at = slice((2 * p + 2) * NODES, (2 * p + 4) * NODES)
        k = 2 * p
        ext[at, EX:] = lane_rows(
            ((0, right[k : k + 1]), (1, right[k + 1 : k + 2]), (126, left[k : k + 1]), (127, left[k + 1 : k + 2]))
        )
        edge[at, :] = lane_rows(((0, right[8 + p : 9 + p]), (127, left[8 + p : 9 + p])))
    cb, ct = below[192:193, :128], above[192:193, :128]
    half = lax.broadcasted_iota(jnp.int32, (1, 128), 1) < NODES
    corner = lane_rows(
        (
            (0, jnp.where(half, pltpu.roll(cb, NODES, 1), ct)),
            (127, jnp.where(half, cb, pltpu.roll(ct, NODES, 1))),
        )
    )
    none = jnp.zeros((NODES, 128), f32)
    ext[: 2 * NODES, :EX] = below[: 2 * NODES]
    ext[: 2 * NODES, EX:] = jnp.concatenate([none, corner[:NODES]], 0)
    ext[10 * NODES :, :EX] = above[: 2 * NODES]
    ext[10 * NODES :, EX:] = jnp.concatenate([corner[NODES:], none], 0)


def fluid_kernel(first, n_xs, *refs):
    where = position()
    src, cf, span_a, span_b, cross_a, cross_b, own, *refs, below, above = refs
    below[...], above[...] = sides(where[0], span_a[...], span_b[...])
    left, right = sides(where[1], cross_a[...], cross_b[...])
    if first:
        disp, *raw, msg, ext, edge, mats, r_scr, v_scr = refs
        d_mid = (left[13:14], disp[...], right[13:14])
        d_bel = (below[194:195, :128], below[194:195, 128:], below[195:196, :128])
        d_abv = (above[194:195, :128], above[194:195, 128:], above[195:196, :128])
        extend(src, cf, below, above, left, right, ext, edge)
        for k, ref in enumerate(raw):
            m = ref[...] if k == 0 else -ref[...]
            high = m.astype(bf16).astype(f32)
            mats[k * NODES : (k + 1) * NODES, :] = jnp.concatenate([high, m - high, high], 1).astype(bf16)
    else:
        dmid, d_a, d_b, ext, edge, mats, msg, r_out, v_out, r_scr, v_scr = refs
        d_mid, d_bel, d_abv = (
            (d[0:1], d[1:2], d[2:3]) for d in (dmid[...], *sides(where[0], d_a[...], d_b[...]))
        )
    i_mid = (left[12:13], own[...], right[12:13])
    i_bel = (below[192:193, 128:], below[193:194, :128], below[193:194, 128:])
    i_abv = (above[192:193, 128:], above[193:194, :128], above[193:194, 128:])

    main, side, row_mask, x_own = forcing(i_mid, d_mid, 0, ES * NODES)
    mid = slice(2 * NODES, 10 * NODES)
    r_scr[mid, :EX] = ext[mid, :EX] + main
    r_scr[mid, EX:] = ext[mid, EX:] + side
    for idx, disp3, shift, at in (
        (i_bel, d_bel, 2 - ES, slice(0, 2 * NODES)),
        (i_abv, d_abv, 0, slice(10 * NODES, 12 * NODES)),
    ):
        main, side, _, _ = forcing(idx, disp3, shift, 2 * NODES)
        r_scr[at, :EX] = ext[at, :EX] + main
        r_scr[at, EX:] = ext[at, EX:] + side

    def product(ref, s, lo, hi):
        x = ref[s * NODES : (s + 1) * NODES, :]
        xh, xl = parts(x)
        return jnp.dot(
            mats[lo * NODES : hi * NODES, :], jnp.concatenate([xh, xh, xl], 0),
            preferred_element_type=f32,
        )

    def base(prod):
        return (
            prod[:NODES]
            + pltpu.roll(prod[3 * NODES : 4 * NODES], 1, 1)
            + pltpu.roll(prod[4 * NODES :], LANES - 1, 1)
        )

    def coef(s):
        if s == 1:
            return jnp.concatenate([below[2 * NODES : 3 * NODES], jnp.zeros((NODES, 128), f32)], 1)
        if s == 10:
            return jnp.concatenate([above[2 * NODES : 3 * NODES], jnp.zeros((NODES, 128), f32)], 1)
        return jnp.concatenate([cf[:, s - 2, :], edge[s * NODES : (s + 1) * NODES, :]], 1)

    lanes = lax.broadcasted_iota(jnp.int32, (1, LANES), 1)
    keep = jnp.where(
        (lanes < EX)
        | ((lanes < EX + 2) & (where[1] < n_xs - 1))
        | ((lanes >= LANES - 2) & (where[1] > 0)),
        1.0,
        0.0,
    ).astype(f32)
    low = product(r_scr, 0, 1, 2)
    pending = None
    for s in range(1, 12):
        if s < 11:
            prod = product(r_scr, s, 0, 5)
            up = prod[2 * NODES : 3 * NODES]
        else:
            up = product(r_scr, s, 2, 3)
        if pending is not None:
            v_scr[(s - 1) * NODES : s * NODES, :] = (pending + up) * keep
        if s < 11:
            pending = coef(s) * r_scr[s * NODES : (s + 1) * NODES, :] + base(prod) + low
            low = prod[NODES : 2 * NODES]

    sums = [jnp.zeros((8, EX), f32) for _ in range(5)]
    low = product(v_scr, 1, 1, 2)[:, :EX]
    pending = None
    for s in range(2, 11):
        if s < 10:
            prod = product(v_scr, s, 0, 5)
            up = prod[2 * NODES : 3 * NODES, :EX]
        else:
            up = product(v_scr, s, 2, 3)[:, :EX]
        if pending is not None:
            at = slice((s - 1) * NODES, s * NODES)
            r, v = r_scr[at, :EX], v_scr[at, :EX]
            w = pending + up - THETA * v
            pairs = ((v, v), (v, w), (w, w), (r, v), (r, w))
            for k, (a, b) in enumerate(pairs):
                sums[k] = sums[k] + jnp.sum((a * b).reshape(8, 8, EX), axis=0)
        if s < 10:
            at = slice(s * NODES, (s + 1) * NODES)
            pending = cf[:, s - 2, :] * v_scr[at, :EX] + base(prod)[:, :EX] + low
            low = prod[NODES : 2 * NODES, :EX]

    lane = lax.broadcasted_iota(jnp.int32, (1, 128), 1)
    gram = jnp.zeros((1, 128), f32)
    for k in range(5):
        total = jnp.sum(jnp.sum(sums[k], axis=0, keepdims=True), axis=1, keepdims=True)
        gram = gram + jnp.where(lane == k, total, 0.0)
    cols = pick(onehot(x_own, EX))
    cols = jnp.concatenate([cols, cols], 0)
    rows = [gram]
    for ref in (r_scr, v_scr):
        hi, lo = parts(ref[mid, :EX])
        found = jnp.dot(jnp.concatenate([hi, lo], 1), cols, preferred_element_type=f32)
        rows.append(jnp.sum(jnp.where(row_mask, found, 0.0), axis=0, keepdims=True))
    msg[...] = jnp.broadcast_to(jnp.concatenate(rows, 1)[None], msg.shape)
    if not first:
        r_out[...] = r_scr[mid, :EX]
        v_out[...] = v_scr[mid, :EX]


def solve(got):
    total = jnp.sum(got[:, 0, :128], axis=0, keepdims=True)
    lane = lax.broadcasted_iota(jnp.int32, (1, 128), 1)
    g11, g12, g22, g1, g2 = (
        jnp.sum(jnp.where(lane == k, total, 0.0), axis=1, keepdims=True) for k in range(5)
    )
    ratio = g12 / g11
    b = (g2 - ratio * g1) / (g22 - ratio * g12)
    a = (g1 - b * g12) / g11
    return a - THETA * b, b


def shell_kernel(got, compliance, disp, *rest):
    out = rest[-1]
    a, b = solve(got)
    start = position()[0] * 16
    traces = a * got[pl.ds(start, 16), 0, 128:256] + b * got[pl.ds(start, 16), 0, 256:]
    acc = jnp.zeros((IFN, 128), f32)
    for j in range(16):
        acc = acc + compliance[:, j * 128 : (j + 1) * 128] * traces[j : j + 1]
    fresh = jnp.sum(acc.T, axis=0, keepdims=True)
    out[...] = 0.5 * fresh + 0.5 * disp[...]
    if len(rest) > 1:
        r, v, fluid, _ = rest
        for s in range(ES):
            at = slice(s * NODES, (s + 1) * NODES)
            fluid[:, s, :] = a * r[at, :] + b * v[at, :]


def call(kernel, name, outs, ins, scratch=(), pinned=True):
    vm = pl.BlockSpec(memory_space=pltpu.VMEM)
    make = pltpu.VMEM if pinned else jax.ShapeDtypeStruct
    return pl.pallas_call(
        kernel,
        out_shape=[make(*o) for o in outs],
        in_specs=[vm] * len(ins),
        out_specs=[vm] * len(outs),
        scratch_shapes=[pltpu.VMEM(x, f32) for x in scratch],
        compiler_params=pltpu.CompilerParams(vmem_limit_bytes=16 << 20),
        name=name,
    )(*(pltpu.with_memory_space_constraint(x, pltpu.VMEM) for x in ins))


def swaps(axis, wrap):
    size = lax.axis_size(axis)
    pairs = [(i, i + 1) for i in range(size - 1)] + ([(size - 1, 0)] if wrap else [])
    return [[p for i, j in pairs[k::2] for p in ((i, j), (j, i))] for k in (0, 1)]


def body(
    source, coefficient, volume_matrix, span_lower, span_upper, cross_lower,
    cross_upper, interface, compliance, start_displacement,
):
    n_xs = lax.axis_size("xs")
    own, disp, rows = interface[0], start_displacement[0], compliance[0]
    mats = [volume_matrix, span_lower, span_upper, cross_lower, cross_upper]
    message, block = ((128, 1, 3 * 128), f32), ((ES * NODES, EX), f32)
    ext, edges = (12 * NODES, LANES), (200, EX)

    def trade(axis, a, b):
        first, second = swaps(axis, axis == "span")
        return [lax.ppermute(a, axis, first), lax.ppermute(b, axis, second)]

    args = [source, coefficient, own, disp]
    far = pl.BlockSpec(memory_space=pl.ANY)
    *packed, own, disp = pl.pallas_call(
        pack_cross,
        out_shape=[pltpu.VMEM((16, 128), f32)] * 2 + [pltpu.VMEM(x.shape, x.dtype) for x in args[2:]],
        in_specs=[far] * 4,
        out_specs=[pl.BlockSpec(memory_space=pltpu.VMEM)] * 4,
        scratch_shapes=[pltpu.VMEM(x.shape, x.dtype) for x in args[:2]]
        + [pltpu.VMEM((128, 128), f32), pltpu.SemaphoreType.DMA((4,))],
        compiler_params=pltpu.CompilerParams(vmem_limit_bytes=16 << 20),
        name="pack_cross",
    )(*(pltpu.with_memory_space_constraint(x, pltpu.HBM) for x in args))
    cross = trade("xs", *packed)
    packed = call(
        pack_span, "pack_span", [(edges, f32)] * 2, [source, coefficient, *cross, own, disp]
    )
    around = [source, coefficient, *trade("span", *packed), *cross, own]

    sent, base, edge, split = call(
        lambda *refs: fluid_kernel(True, n_xs, *refs), "fluid",
        [message, (ext, f32), ((12 * NODES, 128), f32), ((5 * NODES, 3 * NODES), bf16)],
        around + [disp] + mats, [ext, ext, edges, edges],
    )
    got = lax.all_to_all(sent, AXES, 0, 0, tiled=True)
    (disp,) = call(shell_kernel, "shell", [((1, 128), f32)], [got, rows, disp])
    (mid,) = call(join, "join", [((3, 128), f32)], [*trade("xs", disp, disp), disp])
    sent, r, v = call(
        lambda *refs: fluid_kernel(False, n_xs, *refs), "fluid_last", [message, block, block],
        around + [mid, *trade("span", mid, mid), base, edge, split], [ext, ext, edges, edges],
    )
    got = lax.all_to_all(sent, AXES, 0, 0, tiled=True)
    fluid, disp = call(
        shell_kernel, "shell_last", [(source.shape, f32), ((1, 128), f32)],
        [got, rows, disp, r, v], (), False,
    )
    return fluid, disp[None]


def solution(mesh):
    field = P(None, "span", "xs")
    section = P("span", "xs", None)
    return jax.shard_map(
        body,
        mesh=mesh,
        in_specs=(field, field, P(), P(), P(), P(), P(), section, section, section),
        out_specs=(field, section),
        check_vma=False,
    )
```

time: 98 us -> 73.2 us (0.75)
  blocking collectives: 18.6 us -> 45.5 us
  starting transfers between devices: 28.4 us -> 11 us
  local copies, waits for them, and re-layouts: 16.7 us -> 0.04 us
  waiting for transfers between devices: 15.5 us -> 6.36 us
  Pallas kernels: 14.2 us -> 9.36 us
  other arithmetic: 2.88 us -> 0 us
    all_to_all x1 -> x2, blocking collectives: 18.6 us -> 45.5 us  [body(): got = lax.all_to_all(sent, AXES, 0, 0, tiled=True)]
    all_to_all x1 -> x0, starting transfers between devices: 12.1 us -> none  [exchange(): return lax.all_to_all(message, AXES, 0, 0)]
    all_to_all x1 -> x0, waiting for transfers between devices: 10.6 us -> none  [exchange(): return lax.all_to_all(message, AXES, 0, 0)]
    unnamed x37 -> x16, local copies, waits for them, and re-layouts: 6.97 us -> 0.04 us
    ppermute x8, starting transfers between devices: 16.3 us -> 11 us  [trade(): return [lax.ppermute(a, axis, first), lax.ppermute(b, axis, second)]]
    pallas_call x4 -> x7, Pallas kernels: 14.2 us -> 9.36 us  [the longest x6 7.53 us: call(): pl.pallas_call(kernel, out_shape=[make(*o) for o in outs], in_specs=[vm]...]
    transpose x11 -> x0, local copies, waits for them, and re-layouts: 3.94 us -> none  [the longest x5 2.01 us: layers(): return jnp.transpose(field[:, lo:hi, :], (1, 0, 2)).reshape(-1, EX)]
    all_to_all x2 -> x0, local copies, waits for them, and re-layouts: 2.95 us -> none  [exchange(): return lax.all_to_all(message, AXES, 0, 0)]
  transfers between devices with their start and end apart: 9 -> 8, of which waited for: 4 -> 4; matrix products, arithmetic and copies ran while one was open for 5% -> 0% of each run, Pallas kernels for 0% -> 0%
where the time goes in v2:
time: 73.2 us; the launch traced here: 73 us
  blocking collectives  45.5 us (62%)
  starting transfers between devices  11 us (15%)
  Pallas kernels  9.36 us (13%)
  waiting for transfers between devices  6.36 us (9%)
  between operations  0.78 us (1%)
    all_to_all x2, blocking collectives, body(): got = lax.all_to_all(sent, AXES, 0, 0, tiled=True)  45.5 us
    ppermute x8, starting transfers between devices, trade(): return [lax.ppermute(a, axis, first), lax.ppermute(b, axis, second)]  11 us
    pallas_call x6, Pallas kernels, call(): pl.pallas_call(kernel, out_shape=[make(*o) for o in outs], in_specs=[vm]...  7.53 us
    ppermute x8, waiting for transfers between devices, trade(): return [lax.ppermute(a, axis, first), lax.ppermute(b, axis, second)]  6.36 us
    pallas_call x1, Pallas kernels, body(): pl.pallas_call(pack_cross, out_shape=[pltpu.VMEM((16, 128), f32)] * 2 + [...  1.83 us
  transfers between devices with their start and end apart: 8, of which 4 were waited for; matrix products, arithmetic and copies ran while one was open for 0% of the time, Pallas kernels for 0%

profile of v2, /device:TPU:1, one launch (start us, length us, event | category | flops | bytes accessed | tf_op | source)
XLA Modules:
  0.0 73.0 jit_solution(1422714326875880041)
XLA Ops:
  0.6 0.0 copy-start.1
  0.6 0.0 copy-start
  0.7 0.0 copy-start.7
  0.7 0.0 copy-start.6
  0.7 0.0 copy-start.5
  0.7 0.0 copy-start.4
  0.7 0.0 copy-start.3
  0.7 1.8 %pack_cross.1 = (f32[16,128]{1,0:T(8,128)S(1)}, f32[16,128]{1,0:T(8,128)S(1)}, s32[1,128]{1,0:T(1,128)S(1)}, f32[1,128]{1,0:T(1,128)S(1)}) custom-call(f32[64,8,256]{2,1,0:T(8,128)} %refs_0_.3, f32[64,8,256]{2,1,0:T(8,128)} %refs_1_.3, s32[1,128]{1,0:T(1,128)} %bitcast.6, f32[1,128]{1,0:T(1,128)} %bitcast.7), custom_call_target="tpu_custom_call" | custom-call | tf_op jit(solution)/shard_map/pack_cross/pallas_call | solution.py:341
  2.5 2.1 %collective-permute-start = (f32[16,128]{1,0:T(8,128)S(1)}, f32[16,128]{1,0:T(8,128)S(1)}, u32[]{:S(2)}, u32[]{:S(2)}) collective-permute-start(f32[16,128]{1,0:T(8,128)S(1)} %get-tuple-element.17), channel_id=1, source_target_pairs={{0,1},{1,0},{2,3},{3,2},{4,5},{5,4},{6,7},{7,6},{8,9},{9,8},{10,11... | collective-permute-start | bytes 24584 | tf_op jit(solution)/shard_map/ppermute | solution.py:337
  4.7 0.6 collective-permute-start.1
  5.3 0.4 collective-permute-done.cross_a.refs_4_
  5.7 0.0 collective-permute-done.1.cross_b.refs_5_
  5.7 0.0 copy-done.1
  5.7 0.0 copy-done
  5.7 0.2 pack_span.1
  5.9 0.0 copy-start.2
  6.0 2.0 %collective-permute-start.2 = (f32[200,256]{1,0:T(8,128)S(1)}, f32[200,256]{1,0:T(8,128)S(1)}, u32[]{:S(2)}, u32[]{:S(2)}) collective-permute-start(f32[200,256]{1,0:T(8,128)S(1)} %get-tuple-element.21), channel_id=1, source_target_pairs={{0,16},{16,0},{32,48},{48,32},{64,80},{80,64},{96,112},{112,96},{1... | collective-permute-start | bytes 614408 | tf_op jit(solution)/shard_map/ppermute | solution.py:337
  8.0 1.7 %collective-permute-start.3 = (f32[200,256]{1,0:T(8,128)S(1)}, f32[200,256]{1,0:T(8,128)S(1)}, u32[]{:S(2)}, u32[]{:S(2)}) collective-permute-start(f32[200,256]{1,0:T(8,128)S(1)} %get-tuple-element.22), channel_id=1, source_target_pairs={{16,32},{32,16},{48,64},{64,48},{80,96},{96,80},{112,0},{0,112},{1... | collective-permute-start | bytes 614408 | tf_op jit(solution)/shard_map/ppermute | solution.py:337
  9.7 0.0 collective-permute-done.2.refs_2_
  9.7 3.7 %collective-permute-done.3.refs_3_ = f32[200,256]{1,0:T(8,128)S(1)} collective-permute-done((f32[200,256]{1,0:T(8,128)S(1)}, f32[200,256]{1,0:T(8,128)S(1)}, u32[]{:S(2)}, u32[]{:S(2)}) %collective-permute-start.3) | collective-permute-done | bytes 204832 | tf_op jit(solution)/shard_map/ppermute | solution.py:337
  13.5 0.0 copy-done.7
  13.5 0.0 copy-done.6
  13.5 0.0 copy-done.5
  13.5 0.0 copy-done.4
  13.5 0.0 copy-done.3
  13.5 2.9 %fluid.1 = (f32[128,1,384]{2,1,0:T(1,128)S(1)}, f32[768,384]{1,0:T(8,128)S(1)}, f32[768,128]{1,0:T(8,128)S(1)}, bf16[320,192]{1,0:T(8,128)(2,1)S(1)}) custom-call(f32[64,8,256]{2,1,0:T(8,128)S(1)} %copy-done, f32[64,8,256]{2,1,0:T(8,128)S(1)} %copy-done.1, f32[200,256]{1,0:T(8,128)S(1)} %collective-permute-done.2.refs_2_, ...), custom_call_target="tpu_custom_call" | custom-call | tf_op jit(solution)/shard_map/fluid/pallas_call | solution.py:308
  16.4 26.1 %all_to_all.10.got = f32[128,1,384]{2,1,0:T(1,128)S(1)} all-to-all(f32[128,1,384]{2,1,0:T(1,128)S(1)} %get-tuple-element.23), channel_id=1, replica_groups=mesh['span'=8,'xs'=16] {'span','xs'}, dimensions={0} | all-to-all | bytes 393216 | tf_op jit(solution)/shard_map/all_to_all | solution.py:362
  42.4 0.0 copy-done.2
  42.5 0.3 shell.1.d.disp
  42.8 0.7 collective-permute-start.5
  43.4 1.7 %collective-permute-start.4 = (f32[1,128]{1,0:T(1,128)S(1)}, f32[1,128]{1,0:T(1,128)S(1)}, u32[]{:S(2)}, u32[]{:S(2)}) collective-permute-start(f32[1,128]{1,0:T(1,128)S(1)} %shell.1.d.disp), channel_id=1, source_target_pairs={{0,1},{1,0},{2,3},{3,2},{4,5},{5,4},{6,7},{7,6},{8,9},{9,8},{10,11... | collective-permute-start | bytes 1544 | tf_op jit(solution)/shard_map/ppermute | solution.py:337
  45.2 0.0 collective-permute-done.5.cross_b
  45.2 1.0 %collective-permute-done.4.cross_a = f32[1,128]{1,0:T(1,128)S(1)} collective-permute-done((f32[1,128]{1,0:T(1,128)S(1)}, f32[1,128]{1,0:T(1,128)S(1)}, u32[]{:S(2)}, u32[]{:S(2)}) %collective-permute-start.4) | collective-permute-done | bytes 544 | tf_op jit(solution)/shard_map/ppermute | solution.py:337
  46.1 2.1 %collective-permute-start.7 = (f32[3,128]{1,0:T(4,128)S(1)}, f32[3,128]{1,0:T(4,128)S(1)}, u32[]{:S(2)}, u32[]{:S(2)}) collective-permute-start(f32[3,128]{1,0:T(4,128)S(1)} %join.1.refs_7_), channel_id=1, source_target_pairs={{16,32},{32,16},{48,64},{64,48},{80,96},{96,80},{112,0},{0,112},{1... | collective-permute-start | bytes 4616 | tf_op jit(solution)/shard_map/ppermute | solution.py:337
  48.2 0.0 collective-permute-start.6
  48.2 1.3 %collective-permute-done.7.refs_9_ = f32[3,128]{1,0:T(4,128)S(1)} collective-permute-done((f32[3,128]{1,0:T(4,128)S(1)}, f32[3,128]{1,0:T(4,128)S(1)}, u32[]{:S(2)}, u32[]{:S(2)}) %collective-permute-start.7) | collective-permute-done | bytes 1568 | tf_op jit(solution)/shard_map/ppermute | solution.py:337
  49.5 0.0 collective-permute-done.6.refs_8_
  49.5 2.8 %fluid_last.1 = (f32[128,1,384]{2,1,0:T(1,128)S(1)}, f32[512,256]{1,0:T(8,128)S(1)}, f32[512,256]{1,0:T(8,128)S(1)}) custom-call(f32[64,8,256]{2,1,0:T(8,128)S(1)} %copy-done, f32[64,8,256]{2,1,0:T(8,128)S(1)} %copy-done.1, f32[200,256]{1,0:T(8,128)S(1)} %collective-permute-done.2.refs_2_, f32[200,256]{1,0:T(8,128)S(1)} %collective-permute-done.3.refs_3_, ...), custom_call_target="tpu_custom_call" | custom-call | tf_op jit(solution)/shard_map/fluid_last/pallas_call | solution.py:308
  52.3 19.4 %all_to_all.11.got = f32[128,1,384]{2,1,0:T(1,128)S(1)} all-to-all(f32[128,1,384]{2,1,0:T(1,128)S(1)} %get-tuple-element.27), channel_id=1, replica_groups=mesh['span'=8,'xs'=16] {'span','xs'}, dimensions={0} | all-to-all | bytes 393216 | tf_op jit(solution)/shard_map/all_to_all | solution.py:369
  71.7 1.3 %shell_last.1 = (f32[64,8,256]{2,1,0:T(8,128)}, f32[1,128]{1,0:T(1,128)}) custom-call(f32[128,1,384]{2,1,0:T(1,128)S(1)} %all_to_all.11.got, f32[128,2048]{1,0:T(8,128)S(1)} %bitcast.5, f32[1,128]{1,0:T(1,128)S(1)} %shell.1.d.disp, f32[512,256]{1,0:T(8,128)S(1)} %get-tuple-element.28.rest_0_, f32[512,256]{1,0:T(8,128)S(1)} %get-tuple-element.29.rest_1_), custom_call_target="tpu_custom_call" | custom-call | tf_op jit(solution)/shard_map/shell_last/pallas_call | solution.py:308
  (1 shorter events, 0.0 us)
Async XLA Ops:
  0.6 5.1 %copy-start.1 = (f32[64,8,256]{2,1,0:T(8,128)S(1)}, f32[64,8,256]{2,1,0:T(8,128)}, u32[]{:S(2)}) copy-start(f32[64,8,256]{2,1,0:T(8,128)} %refs_1_.3) | copy-start | bytes 1572868
  0.6 5.1 %copy-start = (f32[64,8,256]{2,1,0:T(8,128)S(1)}, f32[64,8,256]{2,1,0:T(8,128)}, u32[]{:S(2)}) copy-start(f32[64,8,256]{2,1,0:T(8,128)} %refs_0_.3) | copy-start | bytes 1572868
  0.7 12.8 %copy-start.7 = (f32[64,64]{1,0:T(8,128)S(1)}, f32[64,64]{1,0:T(8,128)}, u32[]{:S(2)}) copy-start(f32[64,64]{1,0:T(8,128)} %refs_12_.1) | copy-start | bytes 49156
  0.7 12.8 %copy-start.6 = (f32[64,64]{1,0:T(8,128)S(1)}, f32[64,64]{1,0:T(8,128)}, u32[]{:S(2)}) copy-start(f32[64,64]{1,0:T(8,128)} %refs_11_.1) | copy-start | bytes 49156
  0.7 12.8 %copy-start.5 = (f32[64,64]{1,0:T(8,128)S(1)}, f32[64,64]{1,0:T(8,128)}, u32[]{:S(2)}) copy-start(f32[64,64]{1,0:T(8,128)} %refs_10_.1) | copy-start | bytes 49156
  0.7 12.8 %copy-start.4 = (f32[64,64]{1,0:T(8,128)S(1)}, f32[64,64]{1,0:T(8,128)}, u32[]{:S(2)}) copy-start(f32[64,64]{1,0:T(8,128)} %refs_9_.1) | copy-start | bytes 49156
  0.7 12.8 %copy-start.3 = (f32[64,64]{1,0:T(8,128)S(1)}, f32[64,64]{1,0:T(8,128)}, u32[]{:S(2)}) copy-start(f32[64,64]{1,0:T(8,128)} %refs_8_.1) | copy-start | bytes 49156
  2.5 3.1 %collective-permute-start = (f32[16,128]{1,0:T(8,128)S(1)}, f32[16,128]{1,0:T(8,128)S(1)}, u32[]{:S(2)}, u32[]{:S(2)}) collective-permute-start(f32[16,128]{1,0:T(8,128)S(1)} %get-tuple-element.17), channel_id=1, source_target_pairs={{0,1},{1,0},{2,3},{3,2},{4,5},{5,4},{6,7},{7,6},{8,9},{9,8},{10,11... | collective-permute-start | bytes 24584 | tf_op jit(solution)/shard_map/ppermute | solution.py:337
  4.7 1.0 %collective-permute-start.1 = (f32[16,128]{1,0:T(8,128)S(1)}, f32[16,128]{1,0:T(8,128)S(1)}, u32[]{:S(2)}, u32[]{:S(2)}) collective-permute-start(f32[16,128]{1,0:T(8,128)S(1)} %get-tuple-element.18), channel_id=1, source_target_pairs={{1,2},{2,1},{3,4},{4,3},{5,6},{6,5},{7,8},{8,7},{9,10},{10,9},{11,... | collective-permute-start | bytes 24584 | tf_op jit(solution)/shard_map/ppermute | solution.py:337
  5.9 36.5 %copy-start.2 = (f32[1,128,2048]{2,1,0:T(8,128)S(1)}, f32[1,128,2048]{2,1,0:T(8,128)}, u32[]{:S(2)}) copy-start(f32[1,128,2048]{2,1,0:T(8,128)} %param.18) | copy-start | bytes 3145732
  6.0 3.8 %collective-permute-start.2 = (f32[200,256]{1,0:T(8,128)S(1)}, f32[200,256]{1,0:T(8,128)S(1)}, u32[]{:S(2)}, u32[]{:S(2)}) collective-permute-start(f32[200,256]{1,0:T(8,128)S(1)} %get-tuple-element.21), channel_id=1, source_target_pairs={{0,16},{16,0},{32,48},{48,32},{64,80},{80,64},{96,112},{112,96},{1... | collective-permute-start | bytes 614408 | tf_op jit(solution)/shard_map/ppermute | solution.py:337
  8.0 5.5 %collective-permute-start.3 = (f32[200,256]{1,0:T(8,128)S(1)}, f32[200,256]{1,0:T(8,128)S(1)}, u32[]{:S(2)}, u32[]{:S(2)}) collective-permute-start(f32[200,256]{1,0:T(8,128)S(1)} %get-tuple-element.22), channel_id=1, source_target_pairs={{16,32},{32,16},{48,64},{64,48},{80,96},{96,80},{112,0},{0,112},{1... | collective-permute-start | bytes 614408 | tf_op jit(solution)/shard_map/ppermute | solution.py:337
  42.8 2.4 %collective-permute-start.5 = (f32[1,128]{1,0:T(1,128)S(1)}, f32[1,128]{1,0:T(1,128)S(1)}, u32[]{:S(2)}, u32[]{:S(2)}) collective-permute-start(f32[1,128]{1,0:T(1,128)S(1)} %shell.1.d.disp), channel_id=1, source_target_pairs={{1,2},{2,1},{3,4},{4,3},{5,6},{6,5},{7,8},{8,7},{9,10},{10,9},{11,... | collective-permute-start | bytes 1544 | tf_op jit(solution)/shard_map/ppermute | solution.py:337
  43.4 2.7 %collective-permute-start.4 = (f32[1,128]{1,0:T(1,128)S(1)}, f32[1,128]{1,0:T(1,128)S(1)}, u32[]{:S(2)}, u32[]{:S(2)}) collective-permute-start(f32[1,128]{1,0:T(1,128)S(1)} %shell.1.d.disp), channel_id=1, source_target_pairs={{0,1},{1,0},{2,3},{3,2},{4,5},{5,4},{6,7},{7,6},{8,9},{9,8},{10,11... | collective-permute-start | bytes 1544 | tf_op jit(solution)/shard_map/ppermute | solution.py:337
  46.1 3.4 %collective-permute-start.7 = (f32[3,128]{1,0:T(4,128)S(1)}, f32[3,128]{1,0:T(4,128)S(1)}, u32[]{:S(2)}, u32[]{:S(2)}) collective-permute-start(f32[3,128]{1,0:T(4,128)S(1)} %join.1.refs_7_), channel_id=1, source_target_pairs={{16,32},{32,16},{48,64},{64,48},{80,96},{96,80},{112,0},{0,112},{1... | collective-permute-start | bytes 4616 | tf_op jit(solution)/shard_map/ppermute | solution.py:337
  48.2 1.3 %collective-permute-start.6 = (f32[3,128]{1,0:T(4,128)S(1)}, f32[3,128]{1,0:T(4,128)S(1)}, u32[]{:S(2)}, u32[]{:S(2)}) collective-permute-start(f32[3,128]{1,0:T(4,128)S(1)} %join.1.refs_7_), channel_id=1, source_target_pairs={{0,16},{16,0},{32,48},{48,32},{64,80},{80,64},{96,112},{112,96},{1... | collective-permute-start | bytes 4616 | tf_op jit(solution)/shard_map/ppermute | solution.py:337
